TPU v7x, 32 devices: a whole 2x2x4 slice. The times are simulated.
32 devices in a mesh: groups: 2 (over x), tm: 4 (over y, core), tile: 4 (over z).
Axes of the slice: x: 2, y: 2, z: 4, core: 2. Of those that a mesh axis runs over, the one named last changes fastest.
Arguments:
- activations: float32 [24, 8, 64, 384], P(('groups', 'tm'), 'tile'), parts along dimension 0, may hold values from -200 to 200, as said below
- gain_attention: float32 [384], replicated, may hold values from 0.1 to 1.9
- w_query: float32 [384, 384], replicated, may hold values from -10 to 10, as said below
- w_key: float32 [384, 384], replicated, may hold values from -10 to 10, as said below
- w_value: float32 [384, 384], replicated, may hold values from -0.3125 to 0.3125
- w_out: float32 [384, 384], replicated, may hold values from -0.3125 to 0.3125
- gain_conv: float32 [384], replicated, may hold values from 0.1 to 1.9
- conv_weight: float32 [27, 384, 384], P(None, 'tm'), may hold values from -0.0625 to 0.0625
Outputs:
- attended: float32 [24, 8, 64, 384], P(('groups', 'tm'), 'tile'), parts along dimension 0
- conv_out: float32 [24, 8, 64, 384], P(('groups', 'tm'), 'tile'), parts along dimension 0
There are 2 independent parts, one for each index of `groups`. A program takes and returns all parts, laid end to end along the dimension named above; an argument that names none is the same for every part. Nothing has to cross between parts.
Inputs may be any that keep to these rules, and one draw needn't show every extreme that they name: `activations`: finite latent features. `w_query`: finite projection entries. `w_key`: finite projection entries.
All inputs are finite; a program needn't handle non-finite values.
Results may differ from a plain program's by a relative error of at most 0.00023.
Values sent between devices are 32-bit elements; how exact they have to be, the bound alone decides.
A program may use at most 128 MiB of HBM per device.

v0:
```python
import math
import jax
import jax.numpy as jnp
from jax import lax
from jax.sharding import PartitionSpec as P


def from_behind(block, axis, distance):
    devices = range(lax.axis_size(axis))
    route = [(i - distance, i) for i in devices if i - distance in devices]
    return lax.ppermute(block, axis, route)


def padded_2(x, sides, width):
    for axis, dim in sides:
        size, length = (lax.axis_size(axis), x.shape[dim])
        up = [(i, (i + 1) % size) for i in range(size - 1)]
        down = [(j, i) for i, j in up]
        last = lax.slice_in_dim(x, length - width, length, axis=dim)
        leading = lax.slice_in_dim(x, 0, width, axis=dim)
        before = lax.ppermute(last, axis, up)
        after = lax.ppermute(leading, axis, down)
        x = jnp.concatenate([before, x, after], axis=dim)
    return x


def rms_scale(values, gain):
    return values * lax.rsqrt(jnp.mean(values * values, axis=-1, keepdims=True) + 1e-06) * gain


def tap_columns(source, frame_count, row_count, width_cells):
    pieces = []
    for shift_t in range(3):
        for shift_y in range(3):
            for shift_x in range(3):
                pieces.append(
                    source[
                        ...,
                        shift_t : shift_t + frame_count,
                        shift_y : shift_y + row_count,
                        shift_x : shift_x + width_cells,
                        :,
                    ]
                )
    joined = jnp.concatenate(pieces, axis=-1)
    return joined.reshape(-1, joined.shape[-1])


def body(activations, gain_attention, w_query, w_key, w_value, w_out, gain_conv, conv_weight):
    highest = lax.Precision.HIGHEST
    frame_count, row_count, width_cells, channels = activations.shape
    tokens = row_count * width_cells
    pixels = frame_count * tokens
    scale = 1.0 / math.sqrt(channels)
    normed = rms_scale(activations, gain_attention).reshape(pixels, channels)
    queries = jnp.dot(normed, w_query, precision=highest).reshape(frame_count, tokens, channels)
    key_rows = jnp.dot(normed, w_key, precision=highest).reshape(frame_count, tokens, channels)
    values = jnp.dot(normed, w_value, precision=highest).reshape(frame_count, tokens, channels)
    running = jnp.full((frame_count, tokens), -1e30, jnp.float32)
    key_piece = lax.all_gather(key_rows, "tile", axis=1, tiled=True)
    value_piece = lax.all_gather(values, "tile", axis=1, tiled=True)
    scores = jnp.einsum("fqc,fkc->fqk", queries, key_piece, precision=highest) * scale
    largest = jnp.maximum(running, jnp.max(scores, axis=-1))
    powers = jnp.exp(scores - largest[..., None])
    summed = jnp.sum(powers, axis=-1)
    accumulated = jnp.einsum("fqk,fkc->fqc", powers, value_piece, precision=highest)
    running, summed, accumulated = (largest, summed, accumulated)
    mixed = accumulated / summed[..., None]
    attended = activations + jnp.dot(
        mixed.reshape(pixels, channels), w_out, precision=highest
    ).reshape(activations.shape)
    hidden = jax.nn.silu(rms_scale(attended, gain_conv))
    cached = from_behind(hidden[frame_count - 2 :], "tm", 1)
    stacked = jnp.concatenate([cached, hidden], axis=0)
    padded = padded_2(stacked, (("tile", 1),), 1)
    padded = jnp.pad(padded, ((0, 0), (0, 0), (1, 1), (0, 0)))
    piece = lax.all_gather(conv_weight, "tm", axis=1, tiled=True)
    count = piece.shape[1]
    columns = tap_columns(padded, frame_count, row_count, width_cells)
    conv_out = jnp.dot(columns, piece.reshape(27 * count, channels), precision=highest)
    return (attended, conv_out.reshape(activations.shape))


def solution(mesh):
    return jax.shard_map(
        body,
        mesh=mesh,
        in_specs=(
            P(("groups", "tm"), "tile", None, None),
            P(),
            P(),
            P(),
            P(),
            P(),
            P(),
            P(None, "tm", None),
        ),
        out_specs=(
            P(("groups", "tm"), "tile", None, None),
            P(("groups", "tm"), "tile", None, None),
        ),
        check_vma=False,
    )
```

profile of v0, /device:TPU:0, one launch (start us, length us, event | category | flops | bytes accessed | tf_op | source)
XLA Modules:
  0.0 256.4 jit_solution(7575440983940319005)
XLA Ops:
  7.2 1.3 multiply_reduce_fusion.1
  8.5 1.2 multiply_multiply_fusion
  9.7 3.1 %fusion.8 = f32[3,128,384]{2,1,0:T(8,128)} fusion(f32[3,128,384]{2,1,0:T(8,128)S(1)} %bitcast.33, f32[384,384]{1,0:T(8,128)} %param.11), kind=kOutput, calls=%fused_computation.50 | convolution fusion | flops 679477248 | bytes 1769472 | tf_op jit(solution)/shard_map/dot_general | solution.py:57
  13.0 3.1 %fusion.6 = f32[3,128,384]{2,1,0:T(8,128)} fusion(f32[3,128,384]{2,1,0:T(8,128)S(1)} %bitcast.34, f32[384,384]{1,0:T(8,128)} %param.12), kind=kOutput, calls=%fused_computation.48 | convolution fusion | flops 679477248 | bytes 1769472 | tf_op jit(solution)/shard_map/dot_general | solution.py:58
  16.9 2.3 fusion.10
  19.2 47.0 %all-gather.4.cloned.1.call-done = f32[3,512,384]{2,1,0:T(8,128)} async-done(((f32[3,128,384]{2,1,0:T(8,128)}), f32[3,512,384]{2,1,0:T(8,128)}) %all-gather.4.cloned.1.call-update) | async-done | bytes 2359312 | tf_op jit(solution)/shard_map/all_gather | solution.py:60
  66.2 4.3 %fusion.15 = (f32[3,128]{1,0:T(4,128)S(1)}, f32[3,128,512]{2,1,0:T(8,128)S(1)}) fusion(f32[3,128,384]{2,1,0:T(8,128)S(1)} %fusion.10, f32[3,512,384]{2,1,0:T(8,128)} %all-gather.4.cloned.1.call-done), kind=kOutput, calls=%fused_computation.65 | convolution fusion | flops 906362496 | bytes 3737088 | tf_op jit(solution)/shard_map/fqc,fkc->fqk/dot_general | solution.py:62
  70.8 46.9 %all-gather.6.cloned.1.call-done = f32[3,512,384]{2,1,0:T(8,128)} async-done(((f32[3,128,384]{2,1,0:T(8,128)}), f32[3,512,384]{2,1,0:T(8,128)}) %all-gather.6.cloned.1.call-update) | async-done | bytes 2359312 | tf_op jit(solution)/shard_map/all_gather | solution.py:61
  117.7 3.5 %convolution_divide_fusion = f32[3,128,384]{2,1,0:T(8,128)S(1)} fusion(f32[3,512,384]{2,1,0:T(8,128)} %all-gather.6.cloned.1.call-done, f32[3,128,512]{2,1,0:T(8,128)S(1)} %get-tuple-element.7, f32[3,128]{1,0:T(4,128)S(1)} %broadcast_maximum_fusion, f32[3,128]{1,0:T(4,128)S(1)} %fusion.1), kind=kOutput, calls=%fused_computation.16 | convolution fusion | flops 906313728 | bytes 3738624 | tf_op jit(solution)/shard_map/fqk,fkc->fqc/dot_general | solution.py:66
  121.2 1.4 multiply_reduce_fusion
  122.9 1.8 collective-permute-start
  124.7 1.3 collective-permute-done
  126.1 1.6 collective-permute-start.1
  127.7 1.5 collective-permute-start.2
  129.2 4.8 %collective-permute-done.1 = f32[5,1,64,384]{3,2,1,0:T(8,128)S(1)} collective-permute-done((f32[5,1,64,384]{3,2,1,0:T(8,128)S(1)}, f32[5,1,64,384]{3,2,1,0:T(8,128)S(1)}, u32[]{:S(2)}, u32[]{:S(2)}) %collective-permute-start.1) | collective-permute-done | bytes 491552 | tf_op jit(solution)/shard_map/ppermute | solution.py:21
  134.0 4.5 %collective-permute-done.2 = f32[5,1,64,384]{3,2,1,0:T(8,128)S(1)} collective-permute-done((f32[5,1,64,384]{3,2,1,0:T(8,128)S(1)}, f32[5,1,64,384]{3,2,1,0:T(8,128)S(1)}, u32[]{:S(2)}, u32[]{:S(2)}) %collective-permute-start.2) | collective-permute-done | bytes 491552 | tf_op jit(solution)/shard_map/ppermute | solution.py:22
  142.8 0.9 fusion.3
  143.7 1.0 slice_dynamic-update-slice_fusion.19
  154.7 0.9 slice_dynamic-update-slice_fusion.8
  156.5 0.9 slice_dynamic-update-slice_fusion.6
  159.2 1.1 constant_dynamic-update-slice_fusion
  161.3 1.0 slice_dynamic-update-slice_fusion.2
  164.0 55.2 %all-gather.8.cloned.1.call-done = f32[27,384,384]{2,1,0:T(8,128)} async-done(((f32[27,96,384]{2,1,0:T(8,128)}), f32[27,384,384]{2,1,0:T(8,128)}) %all-gather.8.cloned.1.call-update) | async-done | bytes 15925264 | tf_op jit(solution)/shard_map/all_gather | solution.py:77
  219.2 30.7 %fusion.16 = f32[3,2,64,384]{3,2,1,0:T(8,128)} fusion(f32[3,2,64,10368]{3,2,1,0:T(8,128)} %slice_dynamic-update-slice_fusion, f32[10368,384,1,1]{1,0,3,2:T(8,128)} %bitcast.32), kind=kOutput, calls=%fused_computation.66 | convolution fusion | flops 18345885696 | bytes 32440320 | tf_op jit(solution)/shard_map/dot_general | solution.py:80
  (44 shorter events, 21.1 us)
Async XLA Ops:
  7.2 114.0 %copy-start = (f32[384,384]{1,0:T(8,128)S(1)}, f32[384,384]{1,0:T(8,128)}, u32[]{:S(2)}) copy-start(f32[384,384]{1,0:T(8,128)} %param.13) | copy-start | bytes 1769476
  7.2 114.0 %copy-start.1 = (f32[3,2,64,384]{3,2,1,0:T(8,128)S(1)}, f32[3,2,64,384]{3,2,1,0:T(8,128)}, u32[]{:S(2)}) copy-start(f32[3,2,64,384]{3,2,1,0:T(8,128)} %param.8) | copy-start | bytes 1769476
  7.2 115.5 %copy-start.3 = (f32[384]{0:T(512)S(1)}, f32[384]{0:T(512)}, u32[]{:S(2)}) copy-start(f32[384]{0:T(512)} %param.14) | copy-start | bytes 4612
  7.2 59.0 %all-gather.4.cloned.1.call-start = ((), (), s32[]{:S(2)}) async-start(), calls=%async_computation | async-start | bytes 2949120 | tf_op jit(solution)/shard_map/all_gather | solution.py:60
  12.9 104.8 %all-gather.6.cloned.1.call-start = ((), (), s32[]{:S(2)}) async-start(), calls=%async_computation.1 | async-start | bytes 2949120 | tf_op jit(solution)/shard_map/all_gather | solution.py:61
  16.1 203.1 %all-gather.8.cloned.1.call-start = ((), (), s32[]{:S(2)}) async-start(), calls=%async_computation.2 | async-start | bytes 19906560 | tf_op jit(solution)/shard_map/all_gather | solution.py:77
  122.6 36.6 %copy-start.2 = (f32[3,2,64,384]{3,2,1,0:T(8,128)}, f32[3,2,64,384]{3,2,1,0:T(8,128)S(1)}, u32[]{:S(2)}) copy-start(f32[3,2,64,384]{3,2,1,0:T(8,128)S(1)} %get-tuple-element.9) | copy-start | bytes 1769476
  122.9 3.1 %collective-permute-start = (f32[2,2,64,384]{3,2,1,0:T(8,128)S(1)}, f32[2,2,64,384]{3,2,1,0:T(8,128)S(1)}, u32[]{:S(2)}, u32[]{:S(2)}) collective-permute-start(f32[2,2,64,384]{3,2,1,0:T(8,128)S(1)} %slice.135), channel_id=1, source_target_pairs={{0,4},{4,8},{8,12},{1,5},{5,9},{9,13},{2,6},{6,10},{10,14},{3,7},{... | collective-permute-start | bytes 1179656 | tf_op jit(solution)/shard_map/ppermute | solution.py:11
  126.1 8.0 %collective-permute-start.1 = (f32[5,1,64,384]{3,2,1,0:T(8,128)S(1)}, f32[5,1,64,384]{3,2,1,0:T(8,128)S(1)}, u32[]{:S(2)}, u32[]{:S(2)}) collective-permute-start(f32[5,1,64,384]{3,2,1,0:T(8,128)S(1)} %get-tuple-element.4), channel_id=1, source_target_pairs={{0,1},{1,2},{2,3},{4,5},{5,6},{6,7},{8,9},{9,10},{10,11},{12,13},{... | collective-permute-start | bytes 1474568 | tf_op jit(solution)/shard_map/ppermute | solution.py:21
  127.7 10.8 %collective-permute-start.2 = (f32[5,1,64,384]{3,2,1,0:T(8,128)S(1)}, f32[5,1,64,384]{3,2,1,0:T(8,128)S(1)}, u32[]{:S(2)}, u32[]{:S(2)}) collective-permute-start(f32[5,1,64,384]{3,2,1,0:T(8,128)S(1)} %get-tuple-element.5), channel_id=1, source_target_pairs={{1,0},{2,1},{3,2},{5,4},{6,5},{7,6},{9,8},{10,9},{11,10},{13,12},{... | collective-permute-start | bytes 1474568 | tf_op jit(solution)/shard_map/ppermute | solution.py:22
Sparse Core Ops, SparseCore 0:
  13.0 53.1 all-gather.3
  68.3 49.2 all-gather.5
  119.2 99.9 all-gather.7
where the time goes:
time: 257 us; the launch traced here: 256 us
  waiting for transfers between devices  160 us (62%)
  matrix products  48.5 us (19%)
  local copies, waits for them, and re-layouts  22 us (9%)
  between operations  13.9 us (5%)
  other arithmetic  6.63 us (3%)
  starting transfers between devices  5 us (2%)
    all_gather x1, waiting for transfers between devices, body(): piece = lax.all_gather(conv_weight, 'tm', axis=1, tiled=True)  55.2 us
    all_gather x1, waiting for transfers between devices, body(): key_piece = lax.all_gather(key_rows, 'tile', axis=1, tiled=True)  47 us
    all_gather x1, waiting for transfers between devices, body(): value_piece = lax.all_gather(values, 'tile', axis=1, tiled=True)  46.9 us
    dot_general x1, matrix products, body(): jnp.dot(columns, piece.reshape(27 * count, channels), precision=highest)  30.7 us
    unnamed x31, local copies, waits for them, and re-layouts  21 us
  transfers between devices with their start and end apart: 6, of which 6 were waited for; matrix products, arithmetic and copies ran while one was open for 16% of the time, Pallas kernels for 0%

commit v1 on v0

--- a/solution.py
+++ b/solution.py
@@ -58,7 +58,23 @@
     values = jnp.dot(normed, w_value, precision=highest).reshape(frame_count, tokens, channels)
     running = jnp.full((frame_count, tokens), -1e30, jnp.float32)
     key_piece = lax.all_gather(key_rows, "tile", axis=1, tiled=True)
-    value_piece = lax.all_gather(values, "tile", axis=1, tiled=True)
+    ways, here, turn = (lax.axis_size("tile"), lax.axis_index("tile"), values.shape[1])
+    shape = [n * ways if d == 1 else n for d, n in enumerate(values.shape)]
+    full = lax.dynamic_update_slice_in_dim(
+        jnp.zeros(shape, values.dtype), values, here * turn, axis=1
+    )
+    going_up = going_down = values
+    for far in range(1, ways // 2 + 1):
+        going_up = lax.ppermute(going_up, "tile", [(d, (d + 1) % ways) for d in range(ways)])
+        full = lax.dynamic_update_slice_in_dim(full, going_up, (here - far) % ways * turn, axis=1)
+        if 2 * far < ways:
+            going_down = lax.ppermute(
+                going_down, "tile", [(d, (d - 1) % ways) for d in range(ways)]
+            )
+            full = lax.dynamic_update_slice_in_dim(
+                full, going_down, (here + far) % ways * turn, axis=1
+            )
+    value_piece = full
     scores = jnp.einsum("fqc,fkc->fqk", queries, key_piece, precision=highest) * scale
     largest = jnp.maximum(running, jnp.max(scores, axis=-1))
     powers = jnp.exp(scores - largest[..., None])

time: 257 us -> 239 us (0.930)
  waiting for transfers between devices: 160 us -> 113 us
  starting transfers between devices: 5 us -> 29.6 us
  local copies, waits for them, and re-layouts: 22 us -> 25.4 us
    all_gather x1 -> x0, waiting for transfers between devices: 46.9 us -> none  [body(): value_piece = lax.all_gather(values, 'tile', axis=1, tiled=True)]
    ppermute x0 -> x3, waiting for transfers between devices: none -> 46.6 us  [the longest x2 36.7 us: body(): lax.ppermute(going_up, 'tile', [(d, (d + 1) % ways) for d in range(ways)])]
    all_gather x1, waiting for transfers between devices: 47 us -> 4.59 us  [body(): key_piece = lax.all_gather(key_rows, 'tile', axis=1, tiled=True)]
    ppermute x0 -> x3, starting transfers between devices: none -> 24.5 us  [the longest x2 22.5 us: body(): lax.ppermute(going_up, 'tile', [(d, (d + 1) % ways) for d in range(ways)])]
    all_gather x1, waiting for transfers between devices: 55.2 us -> 50.3 us  [body(): piece = lax.all_gather(conv_weight, 'tm', axis=1, tiled=True)]
    dynamic_update_slice x0 -> x3, local copies, waits for them, and re-layouts: none -> 3.31 us  [the longest x2 2.21 us: body(): lax.dynamic_update_slice_in_dim(full, going_up, (here - far) % ways * tur...]
    unnamed x31 -> x29, local copies, waits for them, and re-layouts: 21 us -> 21 us
  transfers between devices with their start and end apart: 6 -> 8, of which waited for: 6 -> 8; matrix products, arithmetic and copies ran while one was open for 16% -> 19% of each run, Pallas kernels for 0% -> 0%
where the time goes in v1:
time: 239 us; the launch traced here: 237 us
  waiting for transfers between devices  113 us (47%)
  matrix products  48.2 us (20%)
  starting transfers between devices  29.6 us (12%)
  local copies, waits for them, and re-layouts  25.4 us (11%)
  between operations  14.2 us (6%)
  other arithmetic  6.52 us (3%)
    all_gather x1, waiting for transfers between devices, body(): piece = lax.all_gather(conv_weight, 'tm', axis=1, tiled=True)  50.3 us
    ppermute x2, waiting for transfers between devices, body(): lax.ppermute(going_up, 'tile', [(d, (d + 1) % ways) for d in range(ways)])  36.7 us
    dot_general x1, matrix products, body(): jnp.dot(columns, piece.reshape(27 * count, channels), precision=highest)  30.7 us
    ppermute x2, starting transfers between devices, body(): lax.ppermute(going_up, 'tile', [(d, (d + 1) % ways) for d in range(ways)])  22.5 us
    unnamed x29, local copies, waits for them, and re-layouts  21 us
    ppermute x1, waiting for transfers between devices, body(): lax.ppermute(going_down, 'tile', [(d, (d - 1) % ways) for d in range(ways)])  9.86 us
    ppermute x1, waiting for transfers between devices, padded_2(): before = lax.ppermute(last, axis, up)  4.82 us
  transfers between devices with their start and end apart: 8, of which 8 were waited for; matrix products, arithmetic and copies ran while one was open for 19% of the time, Pallas kernels for 0%

profile of v1, /device:TPU:0, one launch (start us, length us, event | category | flops | bytes accessed | tf_op | source)
XLA Modules:
  0.0 236.6 jit_solution(10954295819229510925)
XLA Ops:
  7.2 1.2 multiply_reduce_fusion.1
  8.5 1.2 multiply_multiply_fusion
  9.7 3.1 %fusion.8 = f32[3,128,384]{2,1,0:T(8,128)} fusion(f32[3,128,384]{2,1,0:T(8,128)S(1)} %bitcast.35, f32[384,384]{1,0:T(8,128)} %param.11), kind=kOutput, calls=%fused_computation.50 | convolution fusion | flops 679477248 | bytes 1769472 | tf_op jit(solution)/shard_map/dot_general | solution.py:57
  13.8 2.1 constant_dynamic-update-slice_fusion.4
  15.9 3.0 %collective-permute-start = (f32[3,128,384]{2,1,0:T(8,128)}, f32[3,128,384]{2,1,0:T(8,128)}, u32[]{:S(2)}, u32[]{:S(2)}) collective-permute-start(f32[3,128,384]{2,1,0:T(8,128)} %get-tuple-element.7), channel_id=1, source_target_pairs={{0,1},{1,2},{2,3},{3,0},{4,5},{5,6},{6,7},{7,4},{8,9},{9,10},{10,1... | collective-permute-start | bytes 1769480 | tf_op jit(solution)/shard_map/ppermute | solution.py:68
  18.9 2.0 collective-permute-start.1
  20.9 21.7 %collective-permute-done = f32[3,128,384]{2,1,0:T(8,128)} collective-permute-done((f32[3,128,384]{2,1,0:T(8,128)}, f32[3,128,384]{2,1,0:T(8,128)}, u32[]{:S(2)}, u32[]{:S(2)}) %collective-permute-start) | collective-permute-done | bytes 589856 | tf_op jit(solution)/shard_map/ppermute | solution.py:68
  42.6 19.5 %collective-permute-start.2 = (f32[3,128,384]{2,1,0:T(8,128)}, f32[3,128,384]{2,1,0:T(8,128)}, u32[]{:S(2)}, u32[]{:S(2)}) collective-permute-start(f32[3,128,384]{2,1,0:T(8,128)} %collective-permute-done), channel_id=1, source_target_pairs={{0,1},{1,2},{2,3},{3,0},{4,5},{5,6},{6,7},{7,4},{8,9},{9,10},{10,1... | collective-permute-start | bytes 1769480 | tf_op jit(solution)/shard_map/ppermute | solution.py:68
  62.1 3.1 %fusion.10 = f32[3,128,384]{2,1,0:T(8,128)} fusion(f32[3,128,384]{2,1,0:T(8,128)S(1)} %bitcast.37, f32[384,384]{1,0:T(8,128)} %param.10), kind=kOutput, calls=%fused_computation.52 | convolution fusion | flops 679477248 | bytes 1769472 | tf_op jit(solution)/shard_map/dot_general | solution.py:56
  66.4 9.9 %collective-permute-done.1 = f32[3,128,384]{2,1,0:T(8,128)} collective-permute-done((f32[3,128,384]{2,1,0:T(8,128)}, f32[3,128,384]{2,1,0:T(8,128)}, u32[]{:S(2)}, u32[]{:S(2)}) %collective-permute-start.1) | collective-permute-done | bytes 589856 | tf_op jit(solution)/shard_map/ppermute | solution.py:71
  77.3 15.0 %collective-permute-done.2 = f32[3,128,384]{2,1,0:T(8,128)} collective-permute-done((f32[3,128,384]{2,1,0:T(8,128)}, f32[3,128,384]{2,1,0:T(8,128)}, u32[]{:S(2)}, u32[]{:S(2)}) %collective-permute-start.2) | collective-permute-done | bytes 589856 | tf_op jit(solution)/shard_map/ppermute | solution.py:68
  93.5 4.6 %all-gather.3.cloned.1.call-done = f32[3,512,384]{2,1,0:T(8,128)} async-done(((f32[3,128,384]{2,1,0:T(8,128)}), f32[3,512,384]{2,1,0:T(8,128)}) %all-gather.3.cloned.1.call-update) | async-done | bytes 2359312 | tf_op jit(solution)/shard_map/all_gather | solution.py:60
  98.0 4.4 %fusion.15 = (f32[3,128]{1,0:T(4,128)S(1)}, f32[3,128,512]{2,1,0:T(8,128)S(1)}) fusion(f32[3,128,384]{2,1,0:T(8,128)} %fusion.10, f32[3,512,384]{2,1,0:T(8,128)} %all-gather.3.cloned.1.call-done), kind=kOutput, calls=%fused_computation.69 | convolution fusion | flops 906362496 | bytes 3737088 | tf_op jit(solution)/shard_map/fqc,fkc->fqk/dot_general | solution.py:78
  102.8 1.9 convolution_divide_fusion
  104.7 2.8 %multiply_reduce_fusion = (f32[3,2,64]{2,1,0:T(2,128)S(1)}, f32[3,2,64,384]{3,2,1,0:T(8,128)S(1)}) fusion(f32[3,2,64,384]{3,2,1,0:T(8,128)} %param.8, f32[3,2,64,384]{3,2,1,0:T(8,128)S(1)} %bitcast.38, f32[384,384]{1,0:T(8,128)} %param.13), kind=kOutput, calls=%fused_computation.55 | convolution fusion | flops 679919232 | bytes 2360832 | tf_op jit(solution)/shard_map/dot_general | solution.py:85
  107.8 2.0 collective-permute-start.3
  109.8 1.3 collective-permute-done.3
  111.2 1.5 collective-permute-start.4
  112.7 1.5 collective-permute-start.5
  114.2 4.8 %collective-permute-done.4 = f32[5,1,64,384]{3,2,1,0:T(8,128)S(1)} collective-permute-done((f32[5,1,64,384]{3,2,1,0:T(8,128)S(1)}, f32[5,1,64,384]{3,2,1,0:T(8,128)S(1)}, u32[]{:S(2)}, u32[]{:S(2)}) %collective-permute-start.4) | collective-permute-done | bytes 491552 | tf_op jit(solution)/shard_map/ppermute | solution.py:21
  119.0 4.4 %collective-permute-done.5 = f32[5,1,64,384]{3,2,1,0:T(8,128)S(1)} collective-permute-done((f32[5,1,64,384]{3,2,1,0:T(8,128)S(1)}, f32[5,1,64,384]{3,2,1,0:T(8,128)S(1)}, u32[]{:S(2)}, u32[]{:S(2)}) %collective-permute-start.5) | collective-permute-done | bytes 491552 | tf_op jit(solution)/shard_map/ppermute | solution.py:22
  144.0 1.1 constant_dynamic-update-slice_fusion
  148.8 50.3 %all-gather.5.cloned.1.call-done = f32[27,384,384]{2,1,0:T(8,128)} async-done(((f32[27,96,384]{2,1,0:T(8,128)}), f32[27,384,384]{2,1,0:T(8,128)}) %all-gather.5.cloned.1.call-update) | async-done | bytes 15925264 | tf_op jit(solution)/shard_map/all_gather | solution.py:93
  199.1 30.7 %fusion.16 = f32[3,2,64,384]{3,2,1,0:T(8,128)} fusion(f32[3,2,64,10368]{3,2,1,0:T(8,128)} %slice_dynamic-update-slice_fusion, f32[10368,384,1,1]{1,0,3,2:T(8,128)} %bitcast.34), kind=kOutput, calls=%fused_computation.70 | convolution fusion | flops 18345885696 | bytes 32440320 | tf_op jit(solution)/shard_map/dot_general | solution.py:96
  (49 shorter events, 29.2 us)
Async XLA Ops:
  7.2 6.6 %copy-start = (f32[384,384]{1,0:T(8,128)S(1)}, f32[384,384]{1,0:T(8,128)}, u32[]{:S(2)}) copy-start(f32[384,384]{1,0:T(8,128)} %param.12) | copy-start | bytes 1769476
  7.2 100.4 %copy-start.2 = (f32[384]{0:T(512)S(1)}, f32[384]{0:T(512)}, u32[]{:S(2)}) copy-start(f32[384]{0:T(512)} %param.14) | copy-start | bytes 4612
  7.2 90.9 %all-gather.3.cloned.1.call-start = ((), (), s32[]{:S(2)}) async-start(), calls=%async_computation | async-start | bytes 2949120 | tf_op jit(solution)/shard_map/all_gather | solution.py:60
  12.9 186.2 %all-gather.5.cloned.1.call-start = ((), (), s32[]{:S(2)}) async-start(), calls=%async_computation.1 | async-start | bytes 19906560 | tf_op jit(solution)/shard_map/all_gather | solution.py:93
  15.9 26.7 %collective-permute-start = (f32[3,128,384]{2,1,0:T(8,128)}, f32[3,128,384]{2,1,0:T(8,128)}, u32[]{:S(2)}, u32[]{:S(2)}) collective-permute-start(f32[3,128,384]{2,1,0:T(8,128)} %get-tuple-element.7), channel_id=1, source_target_pairs={{0,1},{1,2},{2,3},{3,0},{4,5},{5,6},{6,7},{7,4},{8,9},{9,10},{10,1... | collective-permute-start | bytes 1769480 | tf_op jit(solution)/shard_map/ppermute | solution.py:68
  18.9 57.3 %collective-permute-start.1 = (f32[3,128,384]{2,1,0:T(8,128)}, f32[3,128,384]{2,1,0:T(8,128)}, u32[]{:S(2)}, u32[]{:S(2)}) collective-permute-start(f32[3,128,384]{2,1,0:T(8,128)} %get-tuple-element.7), channel_id=1, source_target_pairs={{0,3},{1,0},{2,1},{3,2},{4,7},{5,4},{6,5},{7,6},{8,11},{9,8},{10,9... | collective-permute-start | bytes 1769480 | tf_op jit(solution)/shard_map/ppermute | solution.py:71
  42.6 49.7 %collective-permute-start.2 = (f32[3,128,384]{2,1,0:T(8,128)}, f32[3,128,384]{2,1,0:T(8,128)}, u32[]{:S(2)}, u32[]{:S(2)}) collective-permute-start(f32[3,128,384]{2,1,0:T(8,128)} %collective-permute-done), channel_id=1, source_target_pairs={{0,1},{1,2},{2,3},{3,0},{4,5},{5,6},{6,7},{7,4},{8,9},{9,10},{10,1... | collective-permute-start | bytes 1769480 | tf_op jit(solution)/shard_map/ppermute | solution.py:68
  107.5 36.5 %copy-start.1 = (f32[3,2,64,384]{3,2,1,0:T(8,128)}, f32[3,2,64,384]{3,2,1,0:T(8,128)S(1)}, u32[]{:S(2)}) copy-start(f32[3,2,64,384]{3,2,1,0:T(8,128)S(1)} %get-tuple-element.11) | copy-start | bytes 1769476
  107.8 3.3 %collective-permute-start.3 = (f32[2,2,64,384]{3,2,1,0:T(8,128)S(1)}, f32[2,2,64,384]{3,2,1,0:T(8,128)S(1)}, u32[]{:S(2)}, u32[]{:S(2)}) collective-permute-start(f32[2,2,64,384]{3,2,1,0:T(8,128)S(1)} %slice.135), channel_id=1, source_target_pairs={{0,4},{4,8},{8,12},{1,5},{5,9},{9,13},{2,6},{6,10},{10,14},{3,7},{... | collective-permute-start | bytes 1179656 | tf_op jit(solution)/shard_map/ppermute | solution.py:11
  111.2 7.8 %collective-permute-start.4 = (f32[5,1,64,384]{3,2,1,0:T(8,128)S(1)}, f32[5,1,64,384]{3,2,1,0:T(8,128)S(1)}, u32[]{:S(2)}, u32[]{:S(2)}) collective-permute-start(f32[5,1,64,384]{3,2,1,0:T(8,128)S(1)} %get-tuple-element.4), channel_id=1, source_target_pairs={{0,1},{1,2},{2,3},{4,5},{5,6},{6,7},{8,9},{9,10},{10,11},{12,13},{... | collective-permute-start | bytes 1474568 | tf_op jit(solution)/shard_map/ppermute | solution.py:21
  112.7 10.7 %collective-permute-start.5 = (f32[5,1,64,384]{3,2,1,0:T(8,128)S(1)}, f32[5,1,64,384]{3,2,1,0:T(8,128)S(1)}, u32[]{:S(2)}, u32[]{:S(2)}) collective-permute-start(f32[5,1,64,384]{3,2,1,0:T(8,128)S(1)} %get-tuple-element.5), channel_id=1, source_target_pairs={{1,0},{2,1},{3,2},{5,4},{6,5},{7,6},{9,8},{10,9},{11,10},{13,12},{... | collective-permute-start | bytes 1474568 | tf_op jit(solution)/shard_map/ppermute | solution.py:22
Sparse Core Ops, SparseCore 0:
  13.0 85.0 all-gather.2
  99.6 99.4 all-gather.4
